TPU v7x, 512 devices: a whole 4x8x8 slice. The times are simulated.
512 devices in a mesh: pair: 16 (over z, core), virt: 32 (over x, y).
Axes of the slice: x: 4, y: 8, z: 8, core: 2. Of those that a mesh axis runs over, the one named last changes fastest.
Arguments:
- amplitudes: bfloat16 [1024, 512, 512], P('pair', 'virt')
- integrals: bfloat16 [8, 512, 512, 512], P(None, 'pair', 'virt')
- pair_occ: int32 [1024, 2], P('virt'), may hold values from 0 to 119, as said below
- occ_irrep: int32 [120], replicated, may hold values from 0 to 7, as said below
- virt_irrep: int32 [512], replicated, may hold values from 0 to 7, as said below
- occ_energy: float32 [120], replicated, may hold values from -3 to -0.5
- virt_energy: float32 [512], replicated, may hold values from 0.3 to 4
Outputs:
- update: float32 [1024, 8, 512], P('virt', None, 'pair')
Inputs may be any that keep to these rules, and one draw needn't show every extreme that they name: `pair_occ`: each row holds i < j, and rows are distinct. `occ_irrep`: labels of the D2h irreps; every label occurs. `virt_irrep`: labels of the D2h irreps; every label occurs.
All inputs are finite; a program needn't handle non-finite values.
Results may differ from a plain program's by a relative error of at most 0.0003.
Values may be sent and summed in bfloat16 or wider, within the bound.
A program may use at most 128 MiB of HBM per device.

v0:
```python
import jax
import jax.numpy as jnp
from jax import lax
from jax.sharding import PartitionSpec as P


def table_lookup(indices, table, zero_value):
    orbital = jnp.arange(table.shape[0], dtype=jnp.int32)
    hits = indices[:, None] == orbital[None, :]
    return jnp.sum(jnp.where(hits, table[None, :], zero_value), axis=1)


def local(amplitudes, integrals, pair_occ, occ_irrep, virt_irrep, occ_energy, virt_energy):
    window_size, local_width, local_depth, full_width = integrals.shape
    integral_matrix = integrals.reshape(window_size * local_width, local_depth * full_width)
    owned_rows = pair_occ.shape[0]
    block_rows = lax.all_gather(amplitudes, "pair", axis=0, tiled=True)
    flattened = block_rows.reshape(block_rows.shape[0], local_depth * full_width)
    partial_value = lax.dot_general(
        flattened, integral_matrix, (((1,), (1,)), ((), ())), preferred_element_type=jnp.float32
    )
    summed = lax.psum(partial_value, "virt")
    ladder = lax.dynamic_slice_in_dim(summed, lax.axis_index("virt") * owned_rows, owned_rows, 0)
    ladder = ladder.reshape(owned_rows, window_size, local_width)
    b_offset = lax.axis_index("pair") * local_width
    local_sym = lax.dynamic_slice_in_dim(virt_irrep, b_offset, local_width, 0)
    local_energy = lax.dynamic_slice_in_dim(virt_energy, b_offset, local_width, 0)
    first_occ = pair_occ[:, 0]
    second_occ = pair_occ[:, 1]
    pair_sym = jnp.bitwise_xor(
        table_lookup(first_occ, occ_irrep, 0), table_lookup(second_occ, occ_irrep, 0)
    )
    pair_energy = table_lookup(first_occ, occ_energy, 0.0) + table_lookup(
        second_occ, occ_energy, 0.0
    )
    window_sym = virt_irrep[:window_size]
    total_sym = jnp.bitwise_xor(
        pair_sym[:, None, None],
        jnp.bitwise_xor(window_sym[None, :, None], local_sym[None, None, :]),
    )
    allowed = total_sym == 0
    denom = (
        pair_energy[:, None, None]
        - virt_energy[:window_size][None, :, None]
        - local_energy[None, None, :]
    )
    return jnp.where(allowed, ladder / denom, jnp.zeros_like(ladder))


def solution(mesh):
    return jax.shard_map(
        local,
        mesh=mesh,
        in_specs=(
            P("pair", "virt", None),
            P(None, "pair", "virt", None),
            P("virt", None),
            P(),
            P(),
            P(),
            P(),
        ),
        out_specs=P("virt", None, "pair"),
        check_vma=False,
    )
```

profile of v0, /device:TPU:64, one launch (start us, length us, event | category | flops | bytes accessed | tf_op | source)
XLA Modules:
  0.0 301.6 jit_solution(1929621240613633479)
XLA Ops:
  6.5 0.0 all-gather.2.cloned.1.call-start
  6.5 0.7 all-gather.2.cloned.1.call-update
  7.3 0.0 all-reduce.2.cloned.1.call-start
  7.3 8.4 %copy.9 = bf16[32,8,16,512]{3,1,2,0:T(8,128)(2,1)} copy(bf16[32,8,16,512]{3,2,1,0:T(8,128)(2,1)} %bitcast.13) | data formatting | bytes 8388608
  15.7 94.0 %all-gather.2.cloned.1.call-done = bf16[1024,16,512]{2,1,0:T(8,128)(2,1)} async-done(((bf16[64,16,512]{2,1,0:T(8,128)(2,1)}), bf16[1024,16,512]{2,1,0:T(8,128)(2,1)}) %all-gather.2.cloned.1.call-update) | async-done | bytes 16777232 | tf_op jit(solution)/shard_map/all_gather | solution.py:17
  109.7 16.0 %copy.8 = bf16[128,8,16,512]{3,1,2,0:T(8,128)(2,1)S(1)} copy(bf16[128,8,16,512]{3,2,1,0:T(8,128)(2,1)} %bitcast.11) | data formatting | bytes 33554432
  125.7 0.0 copy-start.4
  125.7 0.0 copy-start.5
  125.7 0.0 copy-start.1
  125.8 0.0 copy-start.2
  125.8 0.0 copy-start.3
  125.8 0.0 slice-start.1
  125.8 0.0 slice-start
  125.8 0.0 copy-done
  125.8 5.5 %fusion = f32[1024,256]{1,0:T(8,128)} fusion(bf16[1024,8192]{1,0:T(8,128)(2,1)S(1)} %bitcast.12, bf16[256,8192]{1,0:T(8,128)(2,1)S(1)} %bitcast.14), kind=kOutput, calls=%fused_computation.13 | convolution fusion | flops 4294967296 | bytes 22020096 | tf_op jit(solution)/shard_map/dot_general | solution.py:19
  131.4 0.0 all-reduce.2.cloned.1.call-update
  131.4 0.0 copy-done.4
  131.4 0.1 dynamic_slice.11
  131.5 0.0 copy-done.5
  131.5 0.1 dynamic_slice.9
  131.5 0.0 copy-done.1
  131.6 0.0 copy-done.2
  131.6 0.2 select_reduce_fusion
  131.8 0.0 copy-done.3
  131.8 0.2 select_reduce_fusion.2
  132.0 0.1 broadcast_xor_fusion
  132.0 0.0 slice-done
  132.0 0.1 broadcast_subtract_fusion
  132.1 161.0 %all-reduce.2.cloned.1.call-done = f32[1024,256]{1,0:T(8,128)} async-done(((f32[1024,256]{1,0:T(8,128)}), f32[1024,256]{1,0:T(8,128)}) %all-reduce.2.cloned.1.call-update) | async-done | bytes 1048592 | tf_op jit(solution)/shard_map/psum | solution.py:22
  293.1 0.8 constant_dynamic-slice_fusion
  293.9 0.1 reshape.87
  294.0 0.8 divide_select_fusion
  (5 shorter events, 0.0 us)
Async XLA Ops:
  6.5 103.2 %all-gather.2.cloned.1.call-start = ((), (), s32[]{:S(2)}) async-start(), calls=%async_computation | async-start | bytes 17825792 | tf_op jit(solution)/shard_map/all_gather | solution.py:17
  7.3 285.9 %all-reduce.2.cloned.1.call-start = ((), (), s32[]{:S(2)}) async-start(), calls=%async_computation.1 | async-start | bytes 2097152 | tf_op jit(solution)/shard_map/psum | solution.py:22
  109.7 16.1 %copy-start = (bf16[32,8,16,512]{3,1,2,0:T(8,128)(2,1)S(1)}, bf16[32,8,16,512]{3,1,2,0:T(8,128)(2,1)}, u32[]{:S(2)}) copy-start(bf16[32,8,16,512]{3,1,2,0:T(8,128)(2,1)} %copy.9) | copy-start | bytes 12582916
  125.7 5.7 %copy-start.4 = (f32[512]{0:T(512)S(1)}, f32[512]{0:T(512)}, u32[]{:S(2)}) copy-start(f32[512]{0:T(512)} %param.13) | copy-start | bytes 6148
  125.7 5.7 %copy-start.5 = (s32[512]{0:T(512)S(1)}, s32[512]{0:T(512)}, u32[]{:S(2)}) copy-start(s32[512]{0:T(512)} %param.11) | copy-start | bytes 6148
  125.7 5.8 %copy-start.1 = (s32[32,2]{0,1:T(2,128)S(1)}, s32[32,2]{0,1:T(2,128)}, u32[]{:S(2)}) copy-start(s32[32,2]{0,1:T(2,128)} %param.9) | copy-start | bytes 772
  125.8 5.8 %copy-start.2 = (f32[120]{0:T(128)S(1)}, f32[120]{0:T(128)}, u32[]{:S(2)}) copy-start(f32[120]{0:T(128)} %param.12) | copy-start | bytes 1444
  125.8 6.0 %copy-start.3 = (s32[120]{0:T(128)S(1)}, s32[120]{0:T(128)}, u32[]{:S(2)}) copy-start(s32[120]{0:T(128)} %param.10) | copy-start | bytes 1444
  125.8 6.2 %slice-start.1 = ((s32[512]{0:T(512)}), s32[8]{0:T(128)S(1)}, s32[]{:S(2)}) async-start(s32[512]{0:T(512)} %param.11), calls=%async_computation.3 | async-start | bytes 1024 | tf_op jit(solution)/shard_map/slice | solution.py:36
  125.8 6.2 %slice-start = ((f32[512]{0:T(512)}), f32[8]{0:T(128)S(1)}, s32[]{:S(2)}) async-start(f32[512]{0:T(512)} %param.13), calls=%async_computation.2 | async-start | bytes 1024 | tf_op jit(solution)/shard_map/slice | solution.py:44
Sparse Core Ops, SparseCore 0:
  9.4 100.2 all-gather.1
  131.5 161.6 all-reduce.1
where the time goes:
time: 302 us
  waiting for transfers between devices  256 us (85%)
  local copies, waits for them, and re-layouts  25.5 us (8%)
  between operations  13.5 us (4%)
  matrix products  5.53 us (2%)
    psum x1, waiting for transfers between devices, local(): summed = lax.psum(partial_value, 'virt')  161 us
    all_gather x1, waiting for transfers between devices, local(): block_rows = lax.all_gather(amplitudes, 'pair', axis=0, tiled=True)  94 us
    unnamed x14, local copies, waits for them, and re-layouts  24.5 us
  transfers between devices with their start and end apart: 2, of which 2 were waited for; matrix products, arithmetic and copies ran while one was open for 3% of the time, Pallas kernels for 0%

commit v1 on v0

--- a/solution.py
+++ b/solution.py
@@ -19,7 +19,7 @@
     partial_value = lax.dot_general(
         flattened, integral_matrix, (((1,), (1,)), ((), ())), preferred_element_type=jnp.float32
     )
-    summed = lax.psum(partial_value, "virt")
+    summed = jnp.sum(lax.all_gather(partial_value, "virt"), axis=0)
     ladder = lax.dynamic_slice_in_dim(summed, lax.axis_index("virt") * owned_rows, owned_rows, 0)
     ladder = ladder.reshape(owned_rows, window_size, local_width)
     b_offset = lax.axis_index("pair") * local_width

time: 302 us -> 391 us (1.29)
  the two profiles are of different devices: /device:TPU:64 before, /device:TPU:1 now
where the time goes in v1:
time: 391 us; the launch traced here: 390 us
  waiting for transfers between devices  333 us (85%)
  local copies, waits for them, and re-layouts  24.7 us (6%)
  between operations  13.5 us (3%)
  other arithmetic  13.2 us (3%)
  matrix products  5.5 us (1%)
    all_gather x1, waiting for transfers between devices, local(): summed = jnp.sum(lax.all_gather(partial_value, 'virt'), axis=0)  234 us
    all_gather x1, waiting for transfers between devices, local(): block_rows = lax.all_gather(amplitudes, 'pair', axis=0, tiled=True)  98.4 us
    unnamed x14, local copies, waits for them, and re-layouts  24.5 us
    reduce_sum x1, other arithmetic, local(): summed = jnp.sum(lax.all_gather(partial_value, 'virt'), axis=0)  11.9 us
  transfers between devices with their start and end apart: 2, of which 2 were waited for; matrix products, arithmetic and copies ran while one was open for 2% of the time, Pallas kernels for 0%

profile of v1, /device:TPU:1, one launch (start us, length us, event | category | flops | bytes accessed | tf_op | source)
XLA Modules:
  0.0 390.4 jit_solution(478617818500520845)
XLA Ops:
  6.5 0.0 all-gather.4.cloned.1.call-start
  6.5 0.7 all-gather.4.cloned.1.call-update
  7.3 0.0 all-gather.6.cloned.1.call-start
  7.3 8.4 %copy.9 = bf16[32,8,16,512]{3,1,2,0:T(8,128)(2,1)} copy(bf16[32,8,16,512]{3,2,1,0:T(8,128)(2,1)} %bitcast.15) | data formatting | bytes 8388608
  15.7 98.4 %all-gather.4.cloned.1.call-done = bf16[1024,16,512]{2,1,0:T(8,128)(2,1)} async-done(((bf16[64,16,512]{2,1,0:T(8,128)(2,1)}), bf16[1024,16,512]{2,1,0:T(8,128)(2,1)}) %all-gather.4.cloned.1.call-update) | async-done | bytes 16777232 | tf_op jit(solution)/shard_map/all_gather | solution.py:17
  114.2 16.0 %copy.8 = bf16[128,8,16,512]{3,1,2,0:T(8,128)(2,1)S(1)} copy(bf16[128,8,16,512]{3,2,1,0:T(8,128)(2,1)} %bitcast.13) | data formatting | bytes 33554432
  130.2 0.0 copy-start.4
  130.2 0.0 copy-start.5
  130.2 0.0 copy-start.1
  130.2 0.0 copy-start.2
  130.2 0.0 copy-start.3
  130.2 0.0 slice-start.1
  130.2 0.0 slice-start
  130.2 0.0 copy-done
  130.3 5.5 %fusion = f32[1024,256]{1,0:T(8,128)} fusion(bf16[1024,8192]{1,0:T(8,128)(2,1)S(1)} %bitcast.14, bf16[256,8192]{1,0:T(8,128)(2,1)S(1)} %bitcast.16), kind=kOutput, calls=%fused_computation.13 | convolution fusion | flops 4294967296 | bytes 22020096 | tf_op jit(solution)/shard_map/dot_general | solution.py:19
  135.8 0.0 all-gather.6.cloned.1.call-update
  135.8 0.0 copy-done.4
  135.8 0.1 dynamic_slice.11
  135.9 0.0 copy-done.5
  135.9 0.1 dynamic_slice.9
  135.9 0.0 copy-done.1
  136.0 0.0 copy-done.2
  136.0 0.2 select_reduce_fusion
  136.2 0.0 copy-done.3
  136.2 0.2 select_reduce_fusion.2
  136.4 0.0 slice-done.1
  136.4 0.1 broadcast_xor_fusion
  136.4 0.1 broadcast_subtract_fusion
  136.5 234.2 %all-gather.6.cloned.1.call-done = f32[32768,256]{1,0:T(8,128)} async-done(((f32[1024,256]{1,0:T(8,128)}), f32[32768,256]{1,0:T(8,128)}) %all-gather.6.cloned.1.call-update) | async-done | bytes 33554448 | tf_op jit(solution)/shard_map/all_gather | solution.py:22
  370.7 11.9 %reduce_sum.47 = f32[1024,256]{1,0:T(8,128)S(1)} reduce(f32[32,1024,256]{2,1,0:T(8,128)} %bitcast.12, f32[]{:T(128)} %constant.6.clone.1), dimensions={0}, to_apply=%region_2.3 | reduce | flops 8126464 | bytes 34603012 | tf_op jit(solution)/shard_map/reduce_sum | solution.py:22
  382.6 0.1 reshape.87
  382.7 0.8 divide_select_fusion
  (6 shorter events, 0.0 us)
Async XLA Ops:
  6.5 107.6 %all-gather.4.cloned.1.call-start = ((), (), s32[]{:S(2)}) async-start(), calls=%async_computation | async-start | bytes 17825792 | tf_op jit(solution)/shard_map/all_gather | solution.py:17
  7.3 363.4 %all-gather.6.cloned.1.call-start = ((), (), s32[]{:S(2)}) async-start(), calls=%async_computation.1 | async-start | bytes 34603008 | tf_op jit(solution)/shard_map/all_gather | solution.py:22
  114.2 16.1 %copy-start = (bf16[32,8,16,512]{3,1,2,0:T(8,128)(2,1)S(1)}, bf16[32,8,16,512]{3,1,2,0:T(8,128)(2,1)}, u32[]{:S(2)}) copy-start(bf16[32,8,16,512]{3,1,2,0:T(8,128)(2,1)} %copy.9) | copy-start | bytes 12582916
  130.2 5.6 %copy-start.4 = (f32[512]{0:T(512)S(1)}, f32[512]{0:T(512)}, u32[]{:S(2)}) copy-start(f32[512]{0:T(512)} %param.13) | copy-start | bytes 6148
  130.2 5.7 %copy-start.5 = (s32[512]{0:T(512)S(1)}, s32[512]{0:T(512)}, u32[]{:S(2)}) copy-start(s32[512]{0:T(512)} %param.11) | copy-start | bytes 6148
  130.2 5.8 %copy-start.1 = (s32[32,2]{0,1:T(2,128)S(1)}, s32[32,2]{0,1:T(2,128)}, u32[]{:S(2)}) copy-start(s32[32,2]{0,1:T(2,128)} %param.9) | copy-start | bytes 772
  130.2 5.8 %copy-start.2 = (f32[120]{0:T(128)S(1)}, f32[120]{0:T(128)}, u32[]{:S(2)}) copy-start(f32[120]{0:T(128)} %param.12) | copy-start | bytes 1444
  130.2 5.9 %copy-start.3 = (s32[120]{0:T(128)S(1)}, s32[120]{0:T(128)}, u32[]{:S(2)}) copy-start(s32[120]{0:T(128)} %param.10) | copy-start | bytes 1444
  130.2 6.1 %slice-start.1 = ((s32[512]{0:T(512)}), s32[8]{0:T(128)S(1)}, s32[]{:S(2)}) async-start(s32[512]{0:T(512)} %param.11), calls=%async_computation.3 | async-start | bytes 1024 | tf_op jit(solution)/shard_map/slice | solution.py:36
  130.2 6.2 %slice-start = ((f32[512]{0:T(512)}), f32[8]{0:T(128)S(1)}, s32[]{:S(2)}) async-start(f32[512]{0:T(512)} %param.13), calls=%async_computation.2 | async-start | bytes 1024 | tf_op jit(solution)/shard_map/slice | solution.py:44
Sparse Core Ops, SparseCore 0:
  9.4 104.6 all-gather.3
  135.9 234.7 all-gather.5
